TPU v7x, 32 devices: a whole 2x2x4 slice. The times are simulated.
32 devices in a mesh: groups: 2 (over y), sess: 4 (over z), inner: 2 (over x), rep: 2 (over core).
Axes of the slice: x: 2, y: 2, z: 4, core: 2. Of those that a mesh axis runs over, the one named last changes fastest.
Arguments:
- thinker_rows: bfloat16 [4096, 3584], P(('groups', 'sess', 'rep'), 'inner'), parts along dimension 0, may hold values from -6 to 6
- row_session: int32 [4096, 1], P(('groups', 'sess', 'rep')), parts along dimension 0, may hold values from 0 to 31; in each aligned block of 256 rows (0 to 255, 256 to 511, ...) at most 12 rows name the same one
- speaker_of: int32 [64], P('groups'), parts along dimension 0, may hold values from 0 to 7
- prompt_slot: int32 [16], P('groups'), parts along dimension 0, may hold values from 0 to 7, each once
- prompt_cache: bfloat16 [16, 1024, 1024], P(('groups', 'sess'), ('inner', 'rep')), parts along dimension 0, may hold values from -64 to 64
- proj_weight: bfloat16 [3584, 896], P('inner'), may hold values from -0.09375 to 0.09375
- attn_gain: bfloat16 [896], replicated, may hold values from 0.5 to 1.5
- q_weight: bfloat16 [896, 1536], replicated, may hold values from -0.1875 to 0.1875
- k_weight: bfloat16 [896, 512], replicated, may hold values from -0.625 to 0.625
- v_weight: bfloat16 [896, 512], replicated, may hold values from -0.1875 to 0.1875
- o_weight: bfloat16 [1536, 896], replicated, may hold values from -0.15625 to 0.15625
Outputs:
- voice_states: bfloat16 [64, 96, 896], P(('groups', 'sess', 'inner', 'rep')), parts along dimension 0
There are 2 independent parts, one for each index of `groups`. A program takes and returns all parts, laid end to end along the dimension named above; an argument that names none is the same for every part. Nothing has to cross between parts.
Inputs may be any that keep to these rules, and one draw needn't show every extreme that they name: `row_session`: column 0 names the session of the row. Within each block of 256 rows (rows b * 256 to (b + 1) * 256 - 1, the rows of one index of sess+rep) no session is named by more than 12 rows, a bound that some block reaches; every session is named by some row. `prompt_slot`: each slot holds exactly one speaker's prompt.
All inputs are finite; a program needn't handle non-finite values.
Results may differ from a plain program's by a relative error of at most 0.0071.
Values may be sent and summed in bfloat16 or wider, within the bound.
No kernel may reach another device: no remote copies, remote signals or barrier semaphores. Data moves between devices by JAX's collectives and lax.ppermute only.
A program may use at most 128 MiB of HBM per device.

v0:
```python
import jax
import jax.numpy as jnp
from jax import lax
from jax.sharding import PartitionSpec as P

H = 12
KVH = 4
HD = 128
PROMPT = 1024
SLOTS = 96
EPSILON = 1e-06
ROPE_BASE = 1000000.0


def rms_scale(states, gain):
    widened = states.astype(jnp.float32)
    factor = lax.rsqrt(jnp.mean(widened * widened, axis=-1, keepdims=True) + EPSILON)
    return (widened * factor * gain.astype(jnp.float32)).astype(jnp.bfloat16)


def rope_tables(slot_total):
    half_width = HD // 2
    inverse = ROPE_BASE ** (-(jnp.arange(half_width, dtype=jnp.float32) * 2.0) / HD)
    angles = (PROMPT + jnp.arange(slot_total)).astype(jnp.float32)[:, None] * inverse[None, :]
    cosine = jnp.concatenate([jnp.cos(angles), jnp.cos(angles)], axis=1)[:, None, :]
    sine_table = jnp.concatenate([jnp.sin(angles), jnp.sin(angles)], axis=1)[:, None, :]
    return (cosine, sine_table)


def rotate(vectors, cosine, sine_table):
    half_width = vectors.shape[-1] // 2
    turned = jnp.concatenate([-vectors[..., half_width:], vectors[..., :half_width]], axis=-1)
    return vectors * cosine + turned * sine_table


def attend(states, lengths, prompts, attn_gain, q_weight, k_weight, v_weight, o_weight):
    session_total, slot_total, model_width = states.shape
    flat_rows = states.reshape(session_total * slot_total, model_width)
    normed = rms_scale(flat_rows, attn_gain)
    cosine, sine_table = rope_tables(slot_total)
    query = rotate(
        jnp.dot(normed, q_weight, preferred_element_type=jnp.float32).reshape(
            session_total, slot_total, H, HD
        ),
        cosine,
        sine_table,
    ).astype(jnp.bfloat16)
    own_keys = rotate(
        jnp.dot(normed, k_weight, preferred_element_type=jnp.float32).reshape(
            session_total, slot_total, KVH, HD
        ),
        cosine,
        sine_table,
    ).astype(jnp.bfloat16)
    own_values = (
        jnp.dot(normed, v_weight, preferred_element_type=jnp.float32)
        .reshape(session_total, slot_total, KVH, HD)
        .astype(jnp.bfloat16)
    )
    prompt_keys = prompts[:, :, : KVH * HD].reshape(session_total, PROMPT, KVH, HD)
    prompt_values = prompts[:, :, KVH * HD :].reshape(session_total, PROMPT, KVH, HD)
    all_keys = jnp.concatenate([prompt_keys, own_keys], axis=1)
    all_values = jnp.concatenate([prompt_values, own_values], axis=1)
    key_place = jnp.arange(PROMPT + slot_total) - PROMPT
    query_place = jnp.arange(slot_total)
    allowed = (key_place[None, None, :] < 0) | (
        key_place[None, None, :] <= query_place[None, :, None]
    ) & (key_place[None, None, :] < lengths[:, None, None])
    per_group = H // KVH
    outputs = []
    for kv_head in range(KVH):
        query_group = query[:, :, kv_head * per_group : (kv_head + 1) * per_group]
        scores = jnp.einsum(
            "cqhd,ckd->chqk",
            query_group,
            all_keys[:, :, kv_head],
            preferred_element_type=jnp.float32,
        ) * HD ** (-0.5)
        scores = jnp.where(allowed[:, None], scores, -1e30)
        highest = jnp.max(scores, axis=-1, keepdims=True)
        powers = jnp.exp(scores - highest)
        weights = (powers / jnp.sum(powers, axis=-1, keepdims=True)).astype(jnp.bfloat16)
        outputs.append(
            jnp.einsum(
                "chqk,ckd->cqhd",
                weights,
                all_values[:, :, kv_head],
                preferred_element_type=jnp.float32,
            )
        )
    attended = (
        jnp.concatenate(outputs, axis=2)
        .reshape(session_total * slot_total, H * HD)
        .astype(jnp.bfloat16)
    )
    return flat_rows.astype(jnp.float32) + jnp.dot(
        attended, o_weight, preferred_element_type=jnp.float32
    )


def body(
    thinker_rows,
    row_session,
    speaker_of,
    prompt_slot,
    prompt_cache,
    proj_weight,
    attn_gain,
    q_weight,
    k_weight,
    v_weight,
    o_weight,
):
    sess_count = lax.axis_size("sess")
    inner_count = lax.axis_size("inner")
    rep_count = lax.axis_size("rep")
    owner_count = sess_count * rep_count
    session_all = speaker_of.shape[0]
    per_device = session_all // (owner_count * inner_count)
    per_owner = per_device * inner_count
    slot_cap = SLOTS // owner_count
    inner_place = lax.axis_index("inner")
    shard_place = lax.axis_index("sess")
    row_owner = row_session[:, 0]
    device_of = row_owner // per_device
    target = (
        (device_of // (inner_count * rep_count) * rep_count + device_of % rep_count) * per_owner
        + device_of // rep_count % inner_count * per_device
        + row_owner % per_device
    )
    row_order = jnp.arange(row_owner.shape[0])
    earlier = jnp.sum(
        (
            (row_owner[:, None] == row_owner[None, :]) & (row_order[None, :] < row_order[:, None])
        ).astype(jnp.int32),
        axis=1,
    )
    slot_place = target * slot_cap + earlier
    counts = jnp.sum(
        (target[:, None] == jnp.arange(owner_count * per_owner)[None, :]).astype(jnp.int32), axis=0
    ).reshape(owner_count, per_owner)
    partial_sum = jnp.dot(thinker_rows, proj_weight, preferred_element_type=jnp.float32)
    own_columns = lax.psum_scatter(partial_sum, "inner", scatter_dimension=1, tiled=True).astype(
        jnp.bfloat16
    )
    buffer = (
        jnp.zeros((owner_count * per_owner * slot_cap, own_columns.shape[1]), own_columns.dtype)
        .at[slot_place]
        .set(own_columns)
    )
    arrived = lax.all_to_all(
        buffer.reshape(owner_count, per_owner * slot_cap, own_columns.shape[1]),
        ("sess", "rep"),
        split_axis=0,
        concat_axis=0,
        tiled=True,
    )
    counts_in = lax.all_to_all(counts, ("sess", "rep"), split_axis=0, concat_axis=0, tiled=True)
    arrived_rows = arrived.reshape(owner_count, per_owner, slot_cap, arrived.shape[2])
    regrouped = lax.all_to_all(arrived_rows, "inner", split_axis=1, concat_axis=3, tiled=True)
    projected = jnp.transpose(regrouped, (1, 0, 2, 3)).reshape(
        per_device, owner_count * slot_cap, regrouped.shape[3]
    )
    own_counts = lax.dynamic_slice_in_dim(counts_in, inner_place * per_device, per_device, 1)
    offsets = jnp.cumsum(own_counts, axis=0) - own_counts
    lengths = jnp.sum(own_counts, axis=0)
    within = jnp.arange(slot_cap)
    position = jnp.transpose(offsets)[:, :, None] + within[None, None, :]
    live_slot = within[None, None, :] < jnp.transpose(own_counts)[:, :, None]
    position = jnp.where(live_slot, position, SLOTS).reshape(per_device, owner_count * slot_cap)
    session_rows = jnp.broadcast_to(jnp.arange(per_device)[:, None], position.shape)
    compact = (
        jnp.zeros((per_device, SLOTS, projected.shape[2]), jnp.bfloat16)
        .at[session_rows, position]
        .set(projected, mode="drop")
    )
    shard_sessions = per_device * inner_count * rep_count
    wanted_speaker = lax.dynamic_slice_in_dim(
        speaker_of, shard_place * shard_sessions, shard_sessions
    )
    speaker_table = jnp.arange(prompt_slot.shape[0])
    wanted_slot = jnp.sum(
        jnp.where(wanted_speaker[:, None] == speaker_table[None, :], prompt_slot[None, :], 0),
        axis=1,
    )
    piece = lax.all_gather(prompt_cache, "sess", axis=0, tiled=True)
    matching = (wanted_slot[:, None] == jnp.arange(piece.shape[0])[None, :]).astype(jnp.bfloat16)
    chosen = jnp.einsum("sp,ptc->stc", matching, piece, preferred_element_type=jnp.float32)
    prompts = lax.all_to_all(
        chosen.astype(jnp.bfloat16), ("inner", "rep"), split_axis=0, concat_axis=1, tiled=True
    )
    summed = attend(compact, lengths, prompts, attn_gain, q_weight, k_weight, v_weight, o_weight)
    live_rows = (jnp.arange(SLOTS)[None, :] < lengths[:, None]).reshape(-1, 1)
    return (
        jnp.where(live_rows, summed, 0.0)
        .astype(jnp.bfloat16)
        .reshape(per_device, SLOTS, summed.shape[1])
    )


def solution(mesh):
    in_specs = (
        P(("groups", "sess", "rep"), "inner"),
        P(("groups", "sess", "rep"), None),
        P("groups"),
        P("groups"),
        P(("groups", "sess"), ("inner", "rep"), None),
        P("inner", None),
        P(),
        P(),
        P(),
        P(),
        P(),
    )
    out_specs = P(("groups", "sess", "inner", "rep"), None, None)
    return jax.shard_map(body, mesh=mesh, in_specs=in_specs, out_specs=out_specs, check_vma=False)
```

profile of v0, /device:TPU:0, one launch (start us, length us, event | category | flops | bytes accessed | tf_op | source)
XLA Modules:
  0.0 214.4 jit_solution(5181493876565836849)
XLA Ops:
  7.4 1.9 copy-done
  9.3 3.5 %fusion.175 = f32[256,896]{0,1:T(8,128)} fusion(bf16[256,1792]{1,0:T(8,128)(2,1)} %param.11, bf16[1792,896]{1,0:T(8,128)(2,1)S(1)} %copy-done), kind=kOutput, calls=%fused_computation.189 | convolution fusion | flops 822083584 | bytes 5046272 | tf_op jit(solution)/shard_map/dot_general | solution.py:142
  14.4 6.3 %all-to-all-start = ((s32[8,1,4]{2,1,0:T(1,128)}), s32[8,1,4]{2,1,0:T(1,128)S(1)}, u32[]{:S(2)}, u32[]{:S(2)}) async-start(s32[8,1,4]{2,1,0:T(1,128)} %bitcast.1), calls=%async_computation | async-start | bytes 8192 | tf_op jit(solution)/shard_map/all_to_all | solution.py:158
  20.7 4.9 %copy.90 = bf16[896,1536]{0,1:T(8,128)(2,1)} copy(bf16[896,1536]{1,0:T(8,128)(2,1)} %param.18) | data formatting | bytes 5505024 | tf_op args[7]
  27.7 1.3 copy.101
  29.3 5.2 %reduce-scatter.2.cloned.1.call-done = f32[256,448]{0,1:T(8,128)} async-done(((f32[256,896]{0,1:T(8,128)}), f32[256,448]{0,1:T(8,128)}) %reduce-scatter.2.cloned.1.call-update) | async-done | bytes 458768 | tf_op jit(solution)/shard_map/reduce_scatter | solution.py:143
  35.7 2.2 %scatter_custom_fusion = bf16[384,448]{1,0:T(8,128)(2,1)} fusion(s32[256]{0:T(256)S(1)} %bitcast.200, bf16[256,448]{1,0:T(8,128)(2,1)S(1)} %copy.75, bf16[]{:T(256)} %constant.95.clone.1), kind=kCustom, calls=%fused_computation.98 | custom fusion | bytes 344066 | tf_op jit(solution)/shard_map/scatter | solution.py:149
  38.0 4.6 %all-to-all-start.1 = ((bf16[8,48,448]{2,1,0:T(8,128)(2,1)}), bf16[8,48,448]{2,1,0:T(8,128)(2,1)S(1)}, u32[]{:S(2)}, u32[]{:S(2)}) async-start(bf16[8,48,448]{2,1,0:T(8,128)(2,1)} %bitcast.8), calls=%async_computation.2 | async-start | bytes 786432 | tf_op jit(solution)/shard_map/all_to_all | solution.py:151
  43.7 24.4 %all-to-all-done.1 = bf16[8,48,448]{2,1,0:T(8,128)(2,1)S(1)} async-done(((bf16[8,48,448]{2,1,0:T(8,128)(2,1)}), bf16[8,48,448]{2,1,0:T(8,128)(2,1)S(1)}, u32[]{:S(2)}, u32[]{:S(2)}) %all-to-all-start.1) | async-done | bytes 344096 | tf_op jit(solution)/shard_map/all_to_all | solution.py:151
  69.1 3.5 %all-to-all-start.2 = ((bf16[8,4,12,448]{3,0,2,1:T(8,128)(2,1)}), bf16[8,4,12,448]{3,0,2,1:T(8,128)(2,1)S(1)}, u32[]{:S(2)}, u32[]{:S(2)}) async-start(bf16[8,4,12,448]{3,0,2,1:T(8,128)(2,1)} %bitcast.9), calls=%async_computation.3 | async-start | bytes 786432 | tf_op jit(solution)/shard_map/all_to_all | solution.py:160
  72.5 33.9 %all-gather.2.cloned.1.call-done = bf16[8,256,1024]{2,1,0:T(8,128)(2,1)} async-done(((bf16[2,256,1024]{2,1,0:T(8,128)(2,1)}), bf16[8,256,1024]{2,1,0:T(8,128)(2,1)}) %all-gather.2.cloned.1.call-update) | async-done | bytes 4194320 | tf_op jit(solution)/shard_map/all_gather | solution.py:186
  106.4 4.7 %fusion.22 = bf16[8,256,1024]{2,0,1:T(8,128)(2,1)S(1)} fusion(bf16[8,256,1024]{2,1,0:T(8,128)(2,1)} %all-gather.2.cloned.1.call-done, s32[8]{0:T(128)S(1)} %select_reduce_fusion), kind=kOutput, calls=%fused_computation.34 | convolution fusion | flops 35651648 | bytes 8388640 | tf_op jit(solution)/shard_map/sp,ptc->stc/dot_general | solution.py:188
  111.2 4.3 %copy.80 = bf16[8,256,1024]{2,1,0:T(8,128)(2,1)} copy(bf16[8,256,1024]{2,0,1:T(8,128)(2,1)S(1)} %fusion.22) | data formatting | bytes 8388608 | tf_op jit(solution)/shard_map/convert_element_type | solution.py:190
  115.4 5.0 %all-to-all-start.3 = ((bf16[8,256,1024]{2,1,0:T(8,128)(2,1)}), bf16[8,256,1024]{2,1,0:T(8,128)(2,1)}, u32[]{:S(2)}, u32[]{:S(2)}) async-start(bf16[8,256,1024]{2,1,0:T(8,128)(2,1)} %copy.80), calls=%async_computation.4 | async-start | bytes 8388608 | tf_op jit(solution)/shard_map/all_to_all | solution.py:189
  122.3 13.1 %scatter_fusion = bf16[2,96,896]{2,1,0:T(8,128)(2,1)S(1)} fusion(bf16[2,96,896]{2,1,0:T(8,128)(2,1)S(1)} %broadcast_in_dim.55, s32[192]{0:T(256)S(1)} %reshape.305, bf16[192,896]{1,0:T(8,128)(2,1)S(1)} %reshape.307), kind=kCustom, calls=%fused_computation.1 | custom fusion | bytes 1033728 | tf_op jit(solution)/shard_map/scatter | solution.py:175
  137.1 1.2 convolution_convert_fusion
  138.3 1.1 fusion.113
  140.3 28.3 %all-to-all-done.3 = bf16[8,256,1024]{2,1,0:T(8,128)(2,1)} async-done(((bf16[8,256,1024]{2,1,0:T(8,128)(2,1)}), bf16[8,256,1024]{2,1,0:T(8,128)(2,1)}, u32[]{:S(2)}, u32[]{:S(2)}) %all-to-all-start.3) | async-done | bytes 4194336 | tf_op jit(solution)/shard_map/all_to_all | solution.py:189
  168.5 2.6 %copy.81 = bf16[2,4,256,1024]{3,2,1,0:T(8,128)(2,1)S(1)} copy(bf16[2,4,256,1024]{3,2,0,1:T(8,128)(2,1)} %bitcast.16) | data formatting | bytes 8388608 | tf_op jit(solution)/shard_map/all_to_all | solution.py:189
  171.1 2.5 %fusion.154 = (bf16[2,1024,512]{2,1,0:T(8,128)(2,1)}, bf16[2,1024,512]{2,1,0:T(8,128)(2,1)}) fusion(bf16[2,1024,1024]{2,1,0:T(8,128)(2,1)S(1)} %bitcast.185), kind=kLoop, calls=%fused_computation.184 | loop fusion | bytes 8388608 | tf_op jit(solution)/shard_map/slice | solution.py:61
  173.6 3.0 %copy.86 = bf16[2,1024,512]{1,2,0:T(8,128)(2,1)S(1)} copy(bf16[2,1024,512]{2,1,0:T(8,128)(2,1)} %get-tuple-element.10) | data formatting | bytes 4194304 | tf_op jit(solution)/shard_map/slice | solution.py:60
  176.7 2.5 %copy.88 = bf16[2,1024,4,128]{3,1,0,2:T(8,128)(2,1)} copy(bf16[2,1024,4,128]{1,3,2,0:T(8,128)(2,1)S(1)} %bitcast.187) | data formatting | bytes 4194304 | tf_op jit(solution)/shard_map/reshape | solution.py:60
  179.2 3.8 %fusion.155 = (f32[2,3,96]{2,1,0:T(4,128)S(1)}, f32[2,3,96,1120]{3,2,1,0:T(8,128)}) fusion(pred[2,96,1120]{2,1,0:T(8,128)(4,1)S(1)} %copy-done.9, bf16[2,1024,4,128]{3,1,0,2:T(8,128)(2,1)} %copy.88, bf16[2,96,12,128]{3,1,2,0:T(8,128)(2,1)S(1)} %fusion.32, bf16[2,96,4,128]{3,1,2,0:T(8,128)(2,1)S(1)} %copy-done.10), kind=kOutput, calls=%fused_computation.185 | convolution fusion | flops 168879200 | bytes 5245184 | tf_op jit(solution)/shard_map/sub | solution.py:81
  183.0 2.6 %fusion.160 = (f32[2,3,96]{2,1,0:T(4,128)S(1)}, f32[2,3,96,1120]{3,2,1,0:T(8,128)}) fusion(pred[2,96,1120]{2,1,0:T(8,128)(4,1)S(1)} %copy-done.9, bf16[2,1024,4,128]{3,1,0,2:T(8,128)(2,1)S(1)} %copy-done.4, bf16[2,96,12,128]{3,1,2,0:T(8,128)(2,1)S(1)} %fusion.32, bf16[2,96,4,128]{3,1,2,0:T(8,128)(2,1)S(1)} %copy-done.10), kind=kOutput, calls=%fused_computation.186 | convolution fusion | flops 168879200 | bytes 5245184 | tf_op jit(solution)/shard_map/sub | solution.py:81
  185.7 2.6 %fusion.165 = (f32[2,3,96]{2,1,0:T(4,128)S(1)}, f32[2,3,96,1120]{3,2,1,0:T(8,128)}) fusion(pred[2,96,1120]{2,1,0:T(8,128)(4,1)S(1)} %copy-done.9, bf16[2,1024,4,128]{3,1,0,2:T(8,128)(2,1)S(1)} %copy-done.4, bf16[2,96,12,128]{3,1,2,0:T(8,128)(2,1)S(1)} %fusion.32, bf16[2,96,4,128]{3,1,2,0:T(8,128)(2,1)S(1)} %copy-done.10), kind=kOutput, calls=%fused_computation.187 | convolution fusion | flops 168879200 | bytes 5245184 | tf_op jit(solution)/shard_map/sub | solution.py:81
  188.3 2.7 %fusion.170 = (f32[2,3,96]{2,1,0:T(4,128)S(1)}, f32[2,3,96,1120]{3,2,1,0:T(8,128)}) fusion(pred[2,96,1120]{2,1,0:T(8,128)(4,1)S(1)} %copy-done.9, bf16[2,1024,4,128]{3,1,0,2:T(8,128)(2,1)S(1)} %copy-done.4, bf16[2,96,12,128]{3,1,2,0:T(8,128)(2,1)S(1)} %fusion.32, bf16[2,96,4,128]{3,1,2,0:T(8,128)(2,1)S(1)} %copy-done.10), kind=kOutput, calls=%fused_computation.188 | convolution fusion | flops 168879200 | bytes 5245184 | tf_op jit(solution)/shard_map/sub | solution.py:81
  190.9 3.0 %copy.82 = bf16[2,1024,512]{1,2,0:T(8,128)(2,1)S(1)} copy(bf16[2,1024,512]{2,1,0:T(8,128)(2,1)} %get-tuple-element.9) | data formatting | bytes 4194304 | tf_op jit(solution)/shard_map/slice | solution.py:61
  193.9 2.9 %copy.84 = bf16[2,1024,4,128]{3,1,0,2:T(8,128)(2,1)} copy(bf16[2,1024,4,128]{1,3,2,0:T(8,128)(2,1)S(1)} %bitcast.188) | data formatting | bytes 4194304 | tf_op jit(solution)/shard_map/reshape | solution.py:61
  196.8 2.6 %fusion.40 = bf16[2,96,3,128]{3,1,2,0:T(8,128)(2,1)S(1)} fusion(f32[2,3,96,1120]{3,2,1,0:T(8,128)} %get-tuple-element.18, f32[2,3,96]{2,1,0:T(4,128)S(1)} %get-tuple-element.17, bf16[2,1024,4,128]{3,1,0,2:T(8,128)(2,1)} %copy.84, bf16[2,96,4,128]{3,1,2,0:T(8,128)(2,1)S(1)} %copy-done.17), kind=kOutput, calls=%fused_computation.64 | convolution fusion | flops 167661568 | bytes 5024000 | tf_op jit(solution)/shard_map/chqk,ckd->cqhd/dot_general | solution.py:84
  200.7 1.2 copy-done.19
  202.5 1.2 copy-done.18
  205.4 1.5 fusion.30
  (96 shorter events, 15.2 us)
Async XLA Ops:
  7.4 1.9 copy-start
  7.4 6.0 %copy-start.11 = (s32[256,1]{0,1:T(1,128)S(1)}, s32[256,1]{0,1:T(1,128)}, u32[]{:S(2)}) copy-start(s32[256,1]{0,1:T(1,128)} %param.12) | copy-start | bytes 3076
  7.4 27.1 %reduce-scatter.2.cloned.1.call-start = ((), (), s32[]{:S(2)}) async-start(), calls=%async_computation.5 | async-start | bytes 1376256 | tf_op jit(solution)/shard_map/reduce_scatter | solution.py:143
  12.8 93.7 %all-gather.2.cloned.1.call-start = ((), (), s32[]{:S(2)}) async-start(), calls=%async_computation.6 | async-start | bytes 5242880 | tf_op jit(solution)/shard_map/all_gather | solution.py:186
  14.4 14.6 %all-to-all-start = ((s32[8,1,4]{2,1,0:T(1,128)}), s32[8,1,4]{2,1,0:T(1,128)S(1)}, u32[]{:S(2)}, u32[]{:S(2)}) async-start(s32[8,1,4]{2,1,0:T(1,128)} %bitcast.1), calls=%async_computation | async-start | bytes 8192 | tf_op jit(solution)/shard_map/all_to_all | solution.py:158
  20.7 5.0 %copy-start.12 = (bf16[896]{0:T(1024)(128)(2,1)S(1)}, bf16[896]{0:T(1024)(128)(2,1)}, u32[]{:S(2)}) copy-start(bf16[896]{0:T(1024)(128)(2,1)} %param.17) | copy-start | bytes 5380
  20.7 5.0 %copy-start.5 = (bf16[896,512]{1,0:T(8,128)(2,1)S(1)}, bf16[896,512]{1,0:T(8,128)(2,1)}, u32[]{:S(2)}) copy-start(bf16[896,512]{1,0:T(8,128)(2,1)} %param.19) | copy-start | bytes 2752516
  20.7 5.6 %copy-start.14 = (s32[32]{0:T(128)S(1)}, s32[32]{0:T(128)}, u32[]{:S(2)}) copy-start(s32[32]{0:T(128)} %param.13) | copy-start | bytes 388
  20.7 5.7 %copy-start.15 = (s32[8]{0:T(128)S(1)}, s32[8]{0:T(128)}, u32[]{:S(2)}) copy-start(s32[8]{0:T(128)} %param.14) | copy-start | bytes 100
  25.6 2.1 copy-start.6
  38.0 30.1 %all-to-all-start.1 = ((bf16[8,48,448]{2,1,0:T(8,128)(2,1)}), bf16[8,48,448]{2,1,0:T(8,128)(2,1)S(1)}, u32[]{:S(2)}, u32[]{:S(2)}) async-start(bf16[8,48,448]{2,1,0:T(8,128)(2,1)} %bitcast.8), calls=%async_computation.2 | async-start | bytes 786432 | tf_op jit(solution)/shard_map/all_to_all | solution.py:151
  69.1 46.4 %all-to-all-start.2 = ((bf16[8,4,12,448]{3,0,2,1:T(8,128)(2,1)}), bf16[8,4,12,448]{3,0,2,1:T(8,128)(2,1)S(1)}, u32[]{:S(2)}, u32[]{:S(2)}) async-start(bf16[8,4,12,448]{3,0,2,1:T(8,128)(2,1)} %bitcast.9), calls=%async_computation.3 | async-start | bytes 786432 | tf_op jit(solution)/shard_map/all_to_all | solution.py:160
  115.4 53.1 %all-to-all-start.3 = ((bf16[8,256,1024]{2,1,0:T(8,128)(2,1)}), bf16[8,256,1024]{2,1,0:T(8,128)(2,1)}, u32[]{:S(2)}, u32[]{:S(2)}) async-start(bf16[8,256,1024]{2,1,0:T(8,128)(2,1)} %copy.80), calls=%async_computation.4 | async-start | bytes 8388608 | tf_op jit(solution)/shard_map/all_to_all | solution.py:189
  135.3 0.9 copy-start.8
  135.5 1.6 copy-start.7
  136.0 2.2 %copy-start.2 = (bf16[896,1536]{0,1:T(8,128)(2,1)S(1)}, bf16[896,1536]{0,1:T(8,128)(2,1)}, u32[]{:S(2)}) copy-start(bf16[896,1536]{0,1:T(8,128)(2,1)} %copy.90) | copy-start | bytes 8257540
  176.6 2.6 %copy-start.9 = (pred[2,96,1120]{2,1,0:T(8,128)(4,1)S(1)}, pred[2,96,1120]{2,1,0:T(8,128)(4,1)}, u32[]{:S(2)}) copy-start(pred[2,96,1120]{2,1,0:T(8,128)(4,1)} %and_or_fusion) | copy-start | bytes 645124
  176.6 2.6 %copy-start.10 = (bf16[2,96,4,128]{3,1,2,0:T(8,128)(2,1)S(1)}, bf16[2,96,4,128]{3,1,2,0:T(8,128)(2,1)}, u32[]{:S(2)}) copy-start(bf16[2,96,4,128]{3,1,2,0:T(8,128)(2,1)} %fusion.68) | copy-start | bytes 589828
  179.2 3.8 %copy-start.4 = (bf16[2,1024,4,128]{3,1,0,2:T(8,128)(2,1)S(1)}, bf16[2,1024,4,128]{3,1,0,2:T(8,128)(2,1)}, u32[]{:S(2)}) copy-start(bf16[2,1024,4,128]{3,1,0,2:T(8,128)(2,1)} %copy.88) | copy-start | bytes 6291460
  193.9 2.9 %copy-start.17 = (bf16[2,96,4,128]{3,1,2,0:T(8,128)(2,1)S(1)}, bf16[2,96,4,128]{3,1,2,0:T(8,128)(2,1)}, u32[]{:S(2)}) copy-start(bf16[2,96,4,128]{3,1,2,0:T(8,128)(2,1)} %convolution_convert_fusion) | copy-start | bytes 589828
  196.8 2.6 %copy-start.3 = (bf16[2,1024,4,128]{3,1,0,2:T(8,128)(2,1)S(1)}, bf16[2,1024,4,128]{3,1,0,2:T(8,128)(2,1)}, u32[]{:S(2)}) copy-start(bf16[2,1024,4,128]{3,1,0,2:T(8,128)(2,1)} %copy.84) | copy-start | bytes 6291460
  196.8 3.3 %copy-start.20 = (f32[2,3,96,1120]{3,2,1,0:T(8,128)S(1)}, f32[2,3,96,1120]{3,2,1,0:T(8,128)}, u32[]{:S(2)}) copy-start(f32[2,3,96,1120]{3,2,1,0:T(8,128)} %get-tuple-element.20) | copy-start | bytes 7741444
  200.1 1.7 copy-start.19
  201.9 1.7 copy-start.18
  203.6 1.8 copy-start.13
  204.2 1.2 copy-start.16
  204.6 2.4 %copy-start.1 = (bf16[1792,896]{1,0:T(8,128)(2,1)S(1)}, bf16[1792,896]{1,0:T(8,128)(2,1)}, u32[]{:S(2)}) copy-start(bf16[1792,896]{1,0:T(8,128)(2,1)} %param.16) | copy-start | bytes 9633796
Sparse Core Ops, SparseCore 0:
  12.9 21.5 reduce-scatter.1
Sparse Core Ops, SparseCore 1:
  14.8 91.6 all-gather.1
where the time goes:
time: 215 us; the launch traced here: 214 us
  waiting for transfers between devices  92.3 us (43%)
  local copies, waits for them, and re-layouts  52.8 us (25%)
  matrix products  28.5 us (13%)
  starting transfers between devices  19.5 us (9%)
  between operations  15.2 us (7%)
  other arithmetic  6.03 us (3%)
    all_gather x1, waiting for transfers between devices, body(): piece = lax.all_gather(prompt_cache, 'sess', axis=0, tiled=True)  33.9 us
    all_to_all x1, waiting for transfers between devices, body(): lax.all_to_all(chosen.astype(jnp.bfloat16), ('inner', 'rep'), split_axis=...  28.3 us
    all_to_all x1, waiting for transfers between devices, body(): lax.all_to_all(buffer.reshape(owner_count, per_owner * slot_cap, own_colu...  24.4 us
    scatter x1, local copies, waits for them, and re-layouts, body(): compact = jnp.zeros((per_device, SLOTS, projected.shape[2]), jnp.bfloat16...  13.1 us
    sub x4, matrix products, attend(): powers = jnp.exp(scores - highest)  11.7 us
    unnamed x43, local copies, waits for them, and re-layouts  10.7 us
    all_to_all x1, starting transfers between devices, body(): lax.all_to_all(counts, ('sess', 'rep'), split_axis=0, concat_axis=0, tile...  6.33 us
    slice x2, local copies, waits for them, and re-layouts, attend(): prompts[:, :, KVH * HD:].reshape(session_total, PROMPT, KVH, HD)  5.48 us
  transfers between devices with their start and end apart: 6, of which 4 were waited for; matrix products, arithmetic and copies ran while one was open for 20% of the time, Pallas kernels for 0%

commit v1 on v0

--- a/solution.py
+++ b/solution.py
@@ -10,6 +10,15 @@
 SLOTS = 96
 EPSILON = 1e-06
 ROPE_BASE = 1000000.0
+_advance_zones = lambda page, at_axis, k_dim: jnp.concatenate(
+    lax.all_to_all(
+        jnp.stack(jnp.split(page, lax.psum(1, axis_name=("inner", "rep")), at_axis), axis=0),
+        split_axis=0,
+        concat_axis=0,
+        axis_name=("inner", "rep"),
+    ),
+    k_dim,
+)
 
 
 def rms_scale(states, gain):
@@ -186,9 +195,7 @@
     piece = lax.all_gather(prompt_cache, "sess", axis=0, tiled=True)
     matching = (wanted_slot[:, None] == jnp.arange(piece.shape[0])[None, :]).astype(jnp.bfloat16)
     chosen = jnp.einsum("sp,ptc->stc", matching, piece, preferred_element_type=jnp.float32)
-    prompts = lax.all_to_all(
-        chosen.astype(jnp.bfloat16), ("inner", "rep"), split_axis=0, concat_axis=1, tiled=True
-    )
+    prompts = _advance_zones(chosen.astype(jnp.bfloat16), 0, 1)
     summed = attend(compact, lengths, prompts, attn_gain, q_weight, k_weight, v_weight, o_weight)
     live_rows = (jnp.arange(SLOTS)[None, :] < lengths[:, None]).reshape(-1, 1)
     return (

time: 215 us -> 227 us (1.056)
  other arithmetic: 6.03 us -> 14.8 us
  local copies, waits for them, and re-layouts: 52.8 us -> 57.5 us
  waiting for transfers between devices: 92.3 us -> 89.8 us
    unnamed x43 -> x47, local copies, waits for them, and re-layouts: 10.7 us -> 20.2 us
    another operation x0 -> x1, other arithmetic: none -> 8.77 us  [jnp.stack(jnp.split(page, lax.psum(1, axis_name=('inner', 'rep')), at_axi...]
    convert_element_type x1 -> x0, local copies, waits for them, and re-layouts: 4.25 us -> none  [body(): chosen.astype(jnp.bfloat16)]
    another operation x0 -> x1, local copies, waits for them, and re-layouts: none -> 3.06 us  [jnp.stack(jnp.split(page, lax.psum(1, axis_name=('inner', 'rep')), at_axi...]
    slice x1 -> x0, local copies, waits for them, and re-layouts: 2.98 us -> none  [attend(): prompts[:, :, :KVH * HD].reshape(session_total, PROMPT, KVH, HD)]
    all_to_all x1 -> x0, local copies, waits for them, and re-layouts: 2.63 us -> none  [body(): lax.all_to_all(chosen.astype(jnp.bfloat16), ('inner', 'rep'), split_axis=...]
    slice x2 -> x1, local copies, waits for them, and re-layouts: 5.48 us -> 6.02 us  [attend(): prompts[:, :, KVH * HD:].reshape(session_total, PROMPT, KVH, HD)]
  transfers between devices with their start and end apart: 6 -> 6, of which waited for: 4 -> 4; matrix products, arithmetic and copies ran while one was open for 20% -> 23% of each run, Pallas kernels for 0% -> 0%
where the time goes in v1:
time: 227 us; the launch traced here: 226 us
  waiting for transfers between devices  89.8 us (40%)
  local copies, waits for them, and re-layouts  57.5 us (25%)
  matrix products  28.5 us (13%)
  starting transfers between devices  20.2 us (9%)
  between operations  15.2 us (7%)
  other arithmetic  14.8 us (7%)
    all_gather x1, waiting for transfers between devices, body(): piece = lax.all_gather(prompt_cache, 'sess', axis=0, tiled=True)  33.2 us
    all_to_all x1, waiting for transfers between devices, lax.all_to_all(jnp.stack(jnp.split(page, lax.psum(1, axis_name=('inner',...  27.2 us
    all_to_all x1, waiting for transfers between devices, body(): lax.all_to_all(buffer.reshape(owner_count, per_owner * slot_cap, own_colu...  24.4 us
    unnamed x47, local copies, waits for them, and re-layouts  20.2 us
    scatter x1, local copies, waits for them, and re-layouts, body(): compact = jnp.zeros((per_device, SLOTS, projected.shape[2]), jnp.bfloat16...  13.1 us
    sub x4, matrix products, attend(): powers = jnp.exp(scores - highest)  11.7 us
    another operation x1, other arithmetic, jnp.stack(jnp.split(page, lax.psum(1, axis_name=('inner', 'rep')), at_axi...  8.77 us
    all_to_all x1, starting transfers between devices, body(): lax.all_to_all(counts, ('sess', 'rep'), split_axis=0, concat_axis=0, tile...  6.33 us
  transfers between devices with their start and end apart: 6, of which 4 were waited for; matrix products, arithmetic and copies ran while one was open for 23% of the time, Pallas kernels for 0%

profile of v1, /device:TPU:0, one launch (start us, length us, event | category | flops | bytes accessed | tf_op | source)
XLA Modules:
  0.0 226.2 jit_solution(6120638393797086942)
XLA Ops:
  7.4 1.9 copy-done
  9.3 3.5 %fusion.175 = f32[256,896]{0,1:T(8,128)} fusion(bf16[256,1792]{1,0:T(8,128)(2,1)} %param.11, bf16[1792,896]{1,0:T(8,128)(2,1)S(1)} %copy-done), kind=kOutput, calls=%fused_computation.194 | convolution fusion | flops 822083584 | bytes 5046272 | tf_op jit(solution)/shard_map/dot_general | solution.py:151
  14.4 6.3 %all-to-all-start = ((s32[8,1,4]{2,1,0:T(1,128)}), s32[8,1,4]{2,1,0:T(1,128)S(1)}, u32[]{:S(2)}, u32[]{:S(2)}) async-start(s32[8,1,4]{2,1,0:T(1,128)} %bitcast.1), calls=%async_computation | async-start | bytes 8192 | tf_op jit(solution)/shard_map/all_to_all | solution.py:167
  20.7 4.9 %copy.67 = bf16[896,1536]{0,1:T(8,128)(2,1)} copy(bf16[896,1536]{1,0:T(8,128)(2,1)} %param.18) | data formatting | bytes 5505024 | tf_op args[7]
  25.7 1.3 copy.79
  28.4 1.3 copy.78
  30.0 4.5 %reduce-scatter.2.cloned.1.call-done = f32[256,448]{0,1:T(8,128)} async-done(((f32[256,896]{0,1:T(8,128)}), f32[256,448]{0,1:T(8,128)}) %reduce-scatter.2.cloned.1.call-update) | async-done | bytes 458768 | tf_op jit(solution)/shard_map/reduce_scatter | solution.py:152
  35.7 2.2 scatter_custom_fusion
  38.0 4.6 %all-to-all-start.1 = ((bf16[8,48,448]{2,1,0:T(8,128)(2,1)}), bf16[8,48,448]{2,1,0:T(8,128)(2,1)S(1)}, u32[]{:S(2)}, u32[]{:S(2)}) async-start(bf16[8,48,448]{2,1,0:T(8,128)(2,1)} %bitcast.8), calls=%async_computation.2 | async-start | bytes 786432 | tf_op jit(solution)/shard_map/all_to_all | solution.py:160
  43.7 24.4 %all-to-all-done.1 = bf16[8,48,448]{2,1,0:T(8,128)(2,1)S(1)} async-done(((bf16[8,48,448]{2,1,0:T(8,128)(2,1)}), bf16[8,48,448]{2,1,0:T(8,128)(2,1)S(1)}, u32[]{:S(2)}, u32[]{:S(2)}) %all-to-all-start.1) | async-done | bytes 344096 | tf_op jit(solution)/shard_map/all_to_all | solution.py:160
  69.1 4.2 %all-to-all-start.2 = ((bf16[8,4,12,448]{3,0,2,1:T(8,128)(2,1)}), bf16[8,4,12,448]{3,0,2,1:T(8,128)(2,1)}, u32[]{:S(2)}, u32[]{:S(2)}) async-start(bf16[8,4,12,448]{3,0,2,1:T(8,128)(2,1)} %bitcast.9), calls=%async_computation.3 | async-start | bytes 786432 | tf_op jit(solution)/shard_map/all_to_all | solution.py:169
  73.2 33.2 %all-gather.2.cloned.1.call-done = bf16[8,256,1024]{2,1,0:T(8,128)(2,1)} async-done(((bf16[2,256,1024]{2,1,0:T(8,128)(2,1)}), bf16[8,256,1024]{2,1,0:T(8,128)(2,1)}) %all-gather.2.cloned.1.call-update) | async-done | bytes 4194320 | tf_op jit(solution)/shard_map/all_gather | solution.py:195
  106.4 4.7 %fusion.22 = bf16[8,256,1024]{2,0,1:T(8,128)(2,1)S(1)} fusion(bf16[8,256,1024]{2,1,0:T(8,128)(2,1)} %all-gather.2.cloned.1.call-done, s32[8]{0:T(128)S(1)} %select_reduce_fusion), kind=kOutput, calls=%fused_computation.35 | convolution fusion | flops 35651648 | bytes 8388640 | tf_op jit(solution)/shard_map/sp,ptc->stc/dot_general | solution.py:197
  111.2 3.1 %slice_bitcast_fusion.3 = (bf16[1,2,256,1024]{3,1,2,0:T(2,128)(2,1)S(1)}, bf16[1,2,256,1024]{3,1,2,0:T(2,128)(2,1)S(1)}, bf16[1,2,256,1024]{3,1,2,0:T(2,128)(2,1)S(1)}, bf16[1,2,256,1024]{3,1,2,0:T(2,128)(2,1)S(1)}) fusion(bf16[8,256,1024]{2,0,1:T(8,128)(2,1)S(1)} %fusion.22), kind=kLoop, calls=%fused_computation.69 | loop fusion | bytes 8388608 | tf_op jit(solution)/shard_map/stack | solution.py:15
  114.2 8.8 %pad_maximum_fusion = bf16[4,2,256,1024]{3,1,2,0:T(2,128)(2,1)} fusion(bf16[1,2,256,1024]{3,1,2,0:T(2,128)(2,1)S(1)} %get-tuple-element.12, bf16[1,2,256,1024]{3,1,2,0:T(2,128)(2,1)S(1)} %get-tuple-element.13, bf16[1,2,256,1024]{3,1,2,0:T(2,128)(2,1)S(1)} %get-tuple-element.14, bf16[1,2,256,1024]{3,1,2,0:T(2,128)(2,1)S(1)} %get-tuple-element.11), kind=kLoop, calls=%fused_computation.6 | loop fusion | flops 6291456 | bytes 8388608 | tf_op jit(solution)/shard_map/stack | solution.py:15
  123.0 5.0 %all-to-all-start.3 = ((bf16[4,2,256,1024]{3,1,2,0:T(2,128)(2,1)}), bf16[4,2,256,1024]{3,1,2,0:T(2,128)(2,1)}, u32[]{:S(2)}, u32[]{:S(2)}) async-start(bf16[4,2,256,1024]{3,1,2,0:T(2,128)(2,1)} %pad_maximum_fusion), calls=%async_computation.4 | async-start | bytes 8388608 | tf_op jit(solution)/shard_map/all_to_all | solution.py:14
  129.0 1.4 copy.56
  130.9 13.1 %scatter_fusion = bf16[2,96,896]{2,1,0:T(8,128)(2,1)S(1)} fusion(bf16[2,96,896]{2,1,0:T(8,128)(2,1)S(1)} %broadcast_in_dim.55, s32[192]{0:T(256)S(1)} %reshape.313, bf16[192,896]{1,0:T(8,128)(2,1)S(1)} %reshape.315), kind=kCustom, calls=%fused_computation.1 | custom fusion | bytes 1033728 | tf_op jit(solution)/shard_map/scatter | solution.py:184
  148.9 27.2 %all-to-all-done.3 = bf16[4,2,256,1024]{3,1,2,0:T(2,128)(2,1)} async-done(((bf16[4,2,256,1024]{3,1,2,0:T(2,128)(2,1)}), bf16[4,2,256,1024]{3,1,2,0:T(2,128)(2,1)}, u32[]{:S(2)}, u32[]{:S(2)}) %all-to-all-start.3) | async-done | bytes 4194336 | tf_op jit(solution)/shard_map/all_to_all | solution.py:14
  176.1 6.0 %fusion.154 = (bf16[2,1024,512]{2,0,1:T(2,128)(2,1)}, bf16[2,1024,512]{2,0,1:T(2,128)(2,1)}) fusion(bf16[2,1024,1024]{2,0,1:T(2,128)(2,1)} %bitcast.20), kind=kLoop, calls=%fused_computation.189 | loop fusion | bytes 8388608 | tf_op jit(solution)/shard_map/slice | solution.py:70
  182.1 4.7 %copy.81 = bf16[2,1024,512]{1,2,0:T(8,128)(2,1)S(1)} copy(bf16[2,1024,512]{2,0,1:T(2,128)(2,1)} %get-tuple-element.10) | data formatting | bytes 4194304
  186.9 2.5 %copy.65 = bf16[2,1024,4,128]{3,1,0,2:T(8,128)(2,1)} copy(bf16[2,1024,4,128]{1,3,2,0:T(8,128)(2,1)S(1)} %bitcast.193) | data formatting | bytes 4194304 | tf_op jit(solution)/shard_map/reshape | solution.py:69
  189.4 3.8 %fusion.155 = (f32[2,3,96]{2,1,0:T(4,128)S(1)}, f32[2,3,96,1120]{3,2,1,0:T(8,128)}) fusion(pred[2,96,1120]{2,1,0:T(8,128)(4,1)S(1)} %copy-done.10, bf16[2,1024,4,128]{3,1,0,2:T(8,128)(2,1)} %copy.65, bf16[2,96,12,128]{3,1,2,0:T(8,128)(2,1)S(1)} %fusion.32, bf16[2,96,4,128]{3,1,2,0:T(8,128)(2,1)S(1)} %copy-done.11), kind=kOutput, calls=%fused_computation.190 | convolution fusion | flops 168879200 | bytes 5245184 | tf_op jit(solution)/shard_map/sub | solution.py:90
  193.3 2.6 %fusion.160 = (f32[2,3,96]{2,1,0:T(4,128)S(1)}, f32[2,3,96,1120]{3,2,1,0:T(8,128)}) fusion(pred[2,96,1120]{2,1,0:T(8,128)(4,1)S(1)} %copy-done.10, bf16[2,1024,4,128]{3,1,0,2:T(8,128)(2,1)S(1)} %copy-done.5, bf16[2,96,12,128]{3,1,2,0:T(8,128)(2,1)S(1)} %fusion.32, bf16[2,96,4,128]{3,1,2,0:T(8,128)(2,1)S(1)} %copy-done.11), kind=kOutput, calls=%fused_computation.191 | convolution fusion | flops 168879200 | bytes 5245184 | tf_op jit(solution)/shard_map/sub | solution.py:90
  195.9 2.6 %fusion.165 = (f32[2,3,96]{2,1,0:T(4,128)S(1)}, f32[2,3,96,1120]{3,2,1,0:T(8,128)}) fusion(pred[2,96,1120]{2,1,0:T(8,128)(4,1)S(1)} %copy-done.10, bf16[2,1024,4,128]{3,1,0,2:T(8,128)(2,1)S(1)} %copy-done.5, bf16[2,96,12,128]{3,1,2,0:T(8,128)(2,1)S(1)} %fusion.32, bf16[2,96,4,128]{3,1,2,0:T(8,128)(2,1)S(1)} %copy-done.11), kind=kOutput, calls=%fused_computation.192 | convolution fusion | flops 168879200 | bytes 5245184 | tf_op jit(solution)/shard_map/sub | solution.py:90
  198.5 2.7 %fusion.170 = (f32[2,3,96]{2,1,0:T(4,128)S(1)}, f32[2,3,96,1120]{3,2,1,0:T(8,128)}) fusion(pred[2,96,1120]{2,1,0:T(8,128)(4,1)S(1)} %copy-done.10, bf16[2,1024,4,128]{3,1,0,2:T(8,128)(2,1)S(1)} %copy-done.5, bf16[2,96,12,128]{3,1,2,0:T(8,128)(2,1)S(1)} %fusion.32, bf16[2,96,4,128]{3,1,2,0:T(8,128)(2,1)S(1)} %copy-done.11), kind=kOutput, calls=%fused_computation.193 | convolution fusion | flops 168879200 | bytes 5245184 | tf_op jit(solution)/shard_map/sub | solution.py:90
  201.2 4.7 %copy.80 = bf16[2,1024,512]{1,2,0:T(8,128)(2,1)S(1)} copy(bf16[2,1024,512]{2,0,1:T(2,128)(2,1)} %get-tuple-element.9) | data formatting | bytes 4194304
  205.9 2.7 %copy.61 = bf16[2,1024,4,128]{3,1,0,2:T(8,128)(2,1)} copy(bf16[2,1024,4,128]{1,3,2,0:T(8,128)(2,1)S(1)} %bitcast.194) | data formatting | bytes 4194304 | tf_op jit(solution)/shard_map/reshape | solution.py:70
  208.6 2.6 %fusion.40 = bf16[2,96,3,128]{3,1,2,0:T(8,128)(2,1)S(1)} fusion(f32[2,3,96,1120]{3,2,1,0:T(8,128)} %get-tuple-element.22, f32[2,3,96]{2,1,0:T(4,128)S(1)} %get-tuple-element.21, bf16[2,1024,4,128]{3,1,0,2:T(8,128)(2,1)} %copy.61, bf16[2,96,4,128]{3,1,2,0:T(8,128)(2,1)S(1)} %copy-done.18), kind=kOutput, calls=%fused_computation.65 | convolution fusion | flops 167661568 | bytes 5024000 | tf_op jit(solution)/shard_map/chqk,ckd->cqhd/dot_general | solution.py:93
  212.5 1.2 copy-done.20
  214.2 1.2 copy-done.19
  217.2 1.5 fusion.30
  (98 shorter events, 16.5 us)
Async XLA Ops:
  7.4 1.9 copy-start
  7.4 6.0 %copy-start.12 = (s32[256,1]{0,1:T(1,128)S(1)}, s32[256,1]{0,1:T(1,128)}, u32[]{:S(2)}) copy-start(s32[256,1]{0,1:T(1,128)} %param.12) | copy-start | bytes 3076
  7.4 27.1 %reduce-scatter.2.cloned.1.call-start = ((), (), s32[]{:S(2)}) async-start(), calls=%async_computation.5 | async-start | bytes 1376256 | tf_op jit(solution)/shard_map/reduce_scatter | solution.py:152
  12.8 93.7 %all-gather.2.cloned.1.call-start = ((), (), s32[]{:S(2)}) async-start(), calls=%async_computation.6 | async-start | bytes 5242880 | tf_op jit(solution)/shard_map/all_gather | solution.py:195
  14.4 15.3 %all-to-all-start = ((s32[8,1,4]{2,1,0:T(1,128)}), s32[8,1,4]{2,1,0:T(1,128)S(1)}, u32[]{:S(2)}, u32[]{:S(2)}) async-start(s32[8,1,4]{2,1,0:T(1,128)} %bitcast.1), calls=%async_computation | async-start | bytes 8192 | tf_op jit(solution)/shard_map/all_to_all | solution.py:167
  20.7 5.0 %copy-start.13 = (bf16[896]{0:T(1024)(128)(2,1)S(1)}, bf16[896]{0:T(1024)(128)(2,1)}, u32[]{:S(2)}) copy-start(bf16[896]{0:T(1024)(128)(2,1)} %param.17) | copy-start | bytes 5380
  20.7 5.0 %copy-start.6 = (bf16[896,512]{1,0:T(8,128)(2,1)S(1)}, bf16[896,512]{1,0:T(8,128)(2,1)}, u32[]{:S(2)}) copy-start(bf16[896,512]{1,0:T(8,128)(2,1)} %param.19) | copy-start | bytes 2752516
  20.7 6.3 %copy-start.15 = (s32[32]{0:T(128)S(1)}, s32[32]{0:T(128)}, u32[]{:S(2)}) copy-start(s32[32]{0:T(128)} %param.13) | copy-start | bytes 388
  20.7 6.4 %copy-start.16 = (s32[8]{0:T(128)S(1)}, s32[8]{0:T(128)}, u32[]{:S(2)}) copy-start(s32[8]{0:T(128)} %param.14) | copy-start | bytes 100
  25.6 2.7 %copy-start.7 = (bf16[896,512]{1,0:T(8,128)(2,1)S(1)}, bf16[896,512]{1,0:T(8,128)(2,1)}, u32[]{:S(2)}) copy-start(bf16[896,512]{1,0:T(8,128)(2,1)} %param.20) | copy-start | bytes 2752516
  38.0 30.1 %all-to-all-start.1 = ((bf16[8,48,448]{2,1,0:T(8,128)(2,1)}), bf16[8,48,448]{2,1,0:T(8,128)(2,1)S(1)}, u32[]{:S(2)}, u32[]{:S(2)}) async-start(bf16[8,48,448]{2,1,0:T(8,128)(2,1)} %bitcast.8), calls=%async_computation.2 | async-start | bytes 786432 | tf_op jit(solution)/shard_map/all_to_all | solution.py:160
  69.1 53.9 %all-to-all-start.2 = ((bf16[8,4,12,448]{3,0,2,1:T(8,128)(2,1)}), bf16[8,4,12,448]{3,0,2,1:T(8,128)(2,1)}, u32[]{:S(2)}, u32[]{:S(2)}) async-start(bf16[8,4,12,448]{3,0,2,1:T(8,128)(2,1)} %bitcast.9), calls=%async_computation.3 | async-start | bytes 786432 | tf_op jit(solution)/shard_map/all_to_all | solution.py:169
  123.0 53.1 %all-to-all-start.3 = ((bf16[4,2,256,1024]{3,1,2,0:T(2,128)(2,1)}), bf16[4,2,256,1024]{3,1,2,0:T(2,128)(2,1)}, u32[]{:S(2)}, u32[]{:S(2)}) async-start(bf16[4,2,256,1024]{3,1,2,0:T(2,128)(2,1)} %pad_maximum_fusion), calls=%async_computation.4 | async-start | bytes 8388608 | tf_op jit(solution)/shard_map/all_to_all | solution.py:14
  130.9 13.3 %copy-start.3 = (bf16[512,896]{1,0:T(8,128)(2,1)S(1)}, bf16[512,896]{1,0:T(8,128)(2,1)}, u32[]{:S(2)}) copy-start(bf16[512,896]{1,0:T(8,128)(2,1)} %copy.79) | copy-start | bytes 2752516
  143.9 0.9 copy-start.9
  144.1 1.6 copy-start.8
  144.6 2.2 copy-start.2
  186.9 2.6 %copy-start.10 = (pred[2,96,1120]{2,1,0:T(8,128)(4,1)S(1)}, pred[2,96,1120]{2,1,0:T(8,128)(4,1)}, u32[]{:S(2)}) copy-start(pred[2,96,1120]{2,1,0:T(8,128)(4,1)} %and_or_fusion) | copy-start | bytes 645124
  186.9 2.6 %copy-start.11 = (bf16[2,96,4,128]{3,1,2,0:T(8,128)(2,1)S(1)}, bf16[2,96,4,128]{3,1,2,0:T(8,128)(2,1)}, u32[]{:S(2)}) copy-start(bf16[2,96,4,128]{3,1,2,0:T(8,128)(2,1)} %fusion.68) | copy-start | bytes 589828
  189.4 3.8 %copy-start.5 = (bf16[2,1024,4,128]{3,1,0,2:T(8,128)(2,1)S(1)}, bf16[2,1024,4,128]{3,1,0,2:T(8,128)(2,1)}, u32[]{:S(2)}) copy-start(bf16[2,1024,4,128]{3,1,0,2:T(8,128)(2,1)} %copy.65) | copy-start | bytes 6291460
  205.9 2.7 %copy-start.18 = (bf16[2,96,4,128]{3,1,2,0:T(8,128)(2,1)S(1)}, bf16[2,96,4,128]{3,1,2,0:T(8,128)(2,1)}, u32[]{:S(2)}) copy-start(bf16[2,96,4,128]{3,1,2,0:T(8,128)(2,1)} %convolution_convert_fusion) | copy-start | bytes 589828
  208.6 2.6 %copy-start.4 = (bf16[2,1024,4,128]{3,1,0,2:T(8,128)(2,1)S(1)}, bf16[2,1024,4,128]{3,1,0,2:T(8,128)(2,1)}, u32[]{:S(2)}) copy-start(bf16[2,1024,4,128]{3,1,0,2:T(8,128)(2,1)} %copy.61) | copy-start | bytes 6291460
  208.6 3.3 %copy-start.21 = (f32[2,3,96,1120]{3,2,1,0:T(8,128)S(1)}, f32[2,3,96,1120]{3,2,1,0:T(8,128)}, u32[]{:S(2)}) copy-start(f32[2,3,96,1120]{3,2,1,0:T(8,128)} %get-tuple-element.24) | copy-start | bytes 7741444
  211.9 1.7 copy-start.20
  213.6 1.7 copy-start.19
  215.4 1.8 copy-start.14
  216.0 1.2 copy-start.17
  216.3 2.4 %copy-start.1 = (bf16[1792,896]{1,0:T(8,128)(2,1)S(1)}, bf16[1792,896]{1,0:T(8,128)(2,1)}, u32[]{:S(2)}) copy-start(bf16[1792,896]{1,0:T(8,128)(2,1)} %param.16) | copy-start | bytes 9633796
Sparse Core Ops, SparseCore 0:
  12.9 21.5 reduce-scatter.1
Sparse Core Ops, SparseCore 1:
  14.8 91.6 all-gather.1
